TPU v7x, 128 devices: a whole 4x4x4 slice. The times are simulated.
128 devices in a mesh: tm: 16 (over x, z_hi, core), freq: 8 (over y, z_lo).
Axes of the slice: x: 4, y: 4, z: 4 (z_hi: 2, z_lo: 2; z = z_hi * 2 + z_lo), core: 2. Of those that a mesh axis runs over, the one named last changes fastest.
Arguments:
- visibility: bfloat16 [2, 32, 1024, 4096], P(None, None, 'freq', 'tm'), may hold values from -6 to 6
- spectrum_power_sum: float32 [1024, 4096], P('freq', 'tm'), may hold values from 50 to 500, as said below
- square_sum: float32 [1024, 4096], P('freq', 'tm'), as said below
- accum_count: int32 [1024, 4096], P('freq', 'tm'), may hold values from 64 to 256
- rfi_mask: int32 [1024, 4096], P('freq', 'tm'), may hold values 0 or 1
- baseline_delay_class: int32 [32, 1], P('freq'), may hold values from 0 to 3
- filter_bank: bfloat16 [4, 1024, 1024], replicated, may hold values from -0.1875 to 0.1875
Outputs:
- filtered: bfloat16 [2, 32, 1024, 4096], P(None, 'freq', None, 'tm')
Inputs may be any that keep to these rules, and one draw needn't show every extreme that they name: `spectrum_power_sum`: positive in every sample. `square_sum`: positive in every sample.
All inputs are finite; a program needn't handle non-finite values. No bound on the sum of `rfi_mask` on one device may be relied on, other than what follows from the above.
Results may differ from a plain program's by a relative error of at most 0.0043.
The roundings to bfloat16 on the way count: a program that leaves them out, or rounds other values in their place, can miss the bound.
Values may be sent and summed in bfloat16 or wider, within the bound.
A program may use at most 128 MiB of HBM per device.

v0:
```python
import math
import jax
import jax.numpy as jnp
from jax import lax
from jax.sharding import PartitionSpec as P

RIM = 16


def padded_2(value, sides, width):
    for axis, dim in sides:
        devices, length = (lax.axis_size(axis), value.shape[dim])
        up = [(i, (i + 1) % devices) for i in range(devices)]
        down = [(j, i) for i, j in up]
        last = lax.slice_in_dim(value, length - width, length, axis=dim)
        leading = lax.slice_in_dim(value, 0, width, axis=dim)
        before = lax.ppermute(last, axis, up)
        after = lax.ppermute(leading, axis, down)
        value = jnp.concatenate([before, value, after], axis=dim)
    return value


def rotation_table(rows_n, cols_n, period):
    row_index = jnp.arange(rows_n, dtype=jnp.int32)
    col_index = jnp.arange(cols_n, dtype=jnp.int32)
    phase = row_index[:, None] * col_index[None, :] % period
    angles = 2.0 * math.pi / period * phase.astype(jnp.float32)
    cosine = jnp.cos(angles)
    sine = jnp.sin(angles)
    real_row = jnp.stack([cosine, sine])
    imag_row = jnp.stack([-sine, cosine])
    return jnp.stack([real_row, imag_row])


def twist_table(rows_n, cols_n, period):
    row_index = jnp.arange(rows_n, dtype=jnp.int32)
    col_index = jnp.arange(cols_n, dtype=jnp.int32)
    phase = row_index[:, None] * col_index[None, :] % period
    angles = 2.0 * math.pi / period * phase.astype(jnp.float32)
    return (jnp.cos(angles), jnp.sin(angles))


def sidereal_transform(received):
    periods = lax.axis_size("tm")
    samples = received.shape[3]
    inner_len = samples // periods
    base_n = received.shape[1]
    chan_n = received.shape[2]
    widened = received.astype(jnp.float32).reshape(2, base_n, chan_n, periods, inner_len)
    better = lax.Precision.HIGH
    first_table = rotation_table(periods, periods, periods)
    stepped = jnp.einsum("cbfps,dcjp->dbfjs", widened, first_table, precision=better)
    cos_two, sin_two = twist_table(periods, inner_len, samples)
    twist_real = stepped[0] * cos_two + stepped[1] * sin_two
    twist_imag = stepped[1] * cos_two - stepped[0] * sin_two
    twisted = jnp.stack([twist_real, twist_imag])
    tertiary_lookup = rotation_table(inner_len, inner_len, inner_len)
    finished = jnp.einsum("cbfjs,dcks->dbfkj", twisted, tertiary_lookup, precision=better)
    norm_scale = 1.0 / math.sqrt(samples)
    finished = finished.reshape(2, base_n, chan_n, samples) * norm_scale
    return finished.astype(jnp.bfloat16)


def shards(
    visibility,
    spectrum_power_sum,
    square_sum,
    accum_count,
    rfi_mask,
    baseline_delay_class,
    filter_bank,
):
    counts = accum_count.astype(jnp.float32)
    kurtosis = (
        (counts + 1.0)
        / (counts - 1.0)
        * (counts * square_sum / (spectrum_power_sum * spectrum_power_sum) - 1.0)
    )
    flag_weight = rfi_mask.astype(jnp.float32) * jnp.exp(-2.0 * (kurtosis - 1.0) ** 2)
    local_len = flag_weight.shape[1]
    padded = padded_2(flag_weight, (("tm", 1),), RIM)
    smooth_weight = jnp.zeros(flag_weight.shape, jnp.float32)
    for offset in range(2 * RIM + 1):
        factor = (RIM + 1 - abs(offset - RIM)) / float((RIM + 1) ** 2)
        smooth_weight = smooth_weight + factor * padded[:, offset : offset + local_len]
    weighted = (visibility.astype(jnp.float32) * smooth_weight[None, None]).astype(jnp.bfloat16)
    spectrum = sidereal_transform(
        lax.all_to_all(weighted, "tm", split_axis=2, concat_axis=3, tiled=True)
    )
    chosen = jnp.take(filter_bank, baseline_delay_class[:, 0], axis=0)
    moved = lax.all_to_all(spectrum, "tm", split_axis=3, concat_axis=2, tiled=True)
    return jnp.einsum(
        "bgf,cbfm->cbgm",
        chosen,
        lax.all_to_all(moved, "freq", split_axis=1, concat_axis=2, tiled=True),
        preferred_element_type=jnp.float32,
    ).astype(jnp.bfloat16)


def solution(mesh):
    in_specs = (
        P(None, None, "freq", "tm"),
        P("freq", "tm"),
        P("freq", "tm"),
        P("freq", "tm"),
        P("freq", "tm"),
        P("freq", None),
        P(),
    )
    out_specs = P(None, "freq", None, "tm")
    return jax.shard_map(shards, mesh=mesh, in_specs=in_specs, out_specs=out_specs, check_vma=False)
```

profile of v0, /device:TPU:0, one launch (start us, length us, event | category | flops | bytes accessed | tf_op | source)
XLA Modules:
  0.0 342.9 jit_solution(15936010906509529654)
XLA Ops:
  0.0 1.2 exponential_multiply_fusion
  1.2 0.1 fusion.152
  1.3 0.0 collective-permute-start
  1.3 5.7 %collective-permute-start.1 = (f32[128,16]{1,0:T(8,128)S(1)}, f32[128,16]{1,0:T(8,128)S(1)}, u32[]{:S(2)}, u32[]{:S(2)}) collective-permute-start(f32[128,16]{1,0:T(8,128)S(1)} %get-tuple-element.12), channel_id=1, source_target_pairs={{8,0},{16,8},{24,16},{32,24},{40,32},{48,40},{56,48},{64,56},{72,6... | collective-permute-start | bytes 24584 | tf_op jit(solution)/shard_map/ppermute | solution.py:18
  7.0 1.9 collective-permute-done
  8.8 0.0 collective-permute-done.1
  8.9 1.7 fusion.33
  10.6 7.2 %multiply_convert_fusion = bf16[2,32,128,256]{3,1,0,2:T(8,128)(2,1)} fusion(bf16[2,32,128,256]{3,2,1,0:T(8,128)(2,1)} %param.7, f32[128,256]{1,0:T(8,128)S(1)} %fusion.33), kind=kLoop, calls=%fused_computation.13 | loop fusion | flops 6291456 | bytes 8519680 | tf_op jit(solution)/shard_map/convert_element_type | solution.py:86
  17.7 6.8 %all-to-all-start = ((bf16[2,32,128,256]{3,1,0,2:T(8,128)(2,1)}), bf16[2,32,128,256]{3,1,0,2:T(8,128)(2,1)}, u32[]{:S(2)}, u32[]{:S(2)}) async-start(bf16[2,32,128,256]{3,1,0,2:T(8,128)(2,1)} %multiply_convert_fusion), calls=%async_computation | async-start | bytes 8388608 | tf_op jit(solution)/shard_map/all_to_all | solution.py:88
  24.6 0.1 fusion.145
  24.6 0.1 fusion.143
  24.7 0.1 fusion.138
  24.8 1.0 fusion.126
  25.8 1.0 fusion.124
  26.8 0.1 maximum_bitcast_fusion.2
  26.9 50.1 %all-to-all-done = bf16[2,32,128,256]{3,1,0,2:T(8,128)(2,1)} async-done(((bf16[2,32,128,256]{3,1,0,2:T(8,128)(2,1)}), bf16[2,32,128,256]{3,1,0,2:T(8,128)(2,1)}, u32[]{:S(2)}, u32[]{:S(2)}) %all-to-all-start) | async-done | bytes 4194336 | tf_op jit(solution)/shard_map/all_to_all | solution.py:88
  77.0 9.8 %fusion.15 = f32[2,32,8,16,256]{4,3,2,1,0:T(8,128)S(1)} fusion(bf16[2,32,16,8,256]{4,1,0,3,2:T(8,128)(2,1)} %bitcast.8, f32[1,2,16,16]{3,2,1,0:T(8,128)S(1)} %get-tuple-element.14, f32[1,2,16,16]{3,2,1,0:T(8,128)S(1)} %get-tuple-element.13), kind=kOutput, calls=%fused_computation.23 | convolution fusion | flops 402654208 | bytes 12587008 | tf_op jit(solution)/shard_map/cbfps,dcjp->dbfjs/dot_general | solution.py:52
  86.8 1.9 multiply_add_fusion
  88.7 1.8 pad_maximum_fusion
  90.5 11.1 %fusion.10 = bf16[2,32,8,256,16]{3,1,4,2,0:T(8,128)(2,1)} fusion(f32[2,32,8,16,256]{4,3,2,1,0:T(8,128)S(1)} %pad_maximum_fusion, f32[1,2,256,256]{3,2,1,0:T(8,128)S(1)} %get-tuple-element.10, f32[1,2,256,256]{3,2,1,0:T(8,128)S(1)} %get-tuple-element.9), kind=kOutput, calls=%fused_computation.15 | convolution fusion | flops 6446907392 | bytes 13631488 | tf_op jit(solution)/shard_map/cbfjs,dcks->dbfkj/dot_general | solution.py:58
  101.6 23.2 %copy.33 = bf16[2,32,8,256,16]{1,2,0,4,3:T(8,128)(2,1)} copy(bf16[2,32,8,256,16]{3,1,4,2,0:T(8,128)(2,1)} %fusion.10) | data formatting | bytes 8388608 | tf_op jit(solution)/shard_map/convert_element_type | solution.py:61
  124.8 20.7 %reshape.226 = bf16[16,2,65536]{2,1,0:T(2,128)(2,1)} reshape(bf16[4096,2,8,32]{3,2,1,0:T(8,128)(2,1)} %bitcast.74) | data formatting | bytes 8388608
  145.5 65.0 %all_to_all.51 = bf16[16,2,65536]{2,1,0:T(2,128)(2,1)} all-to-all(bf16[16,2,65536]{2,1,0:T(2,128)(2,1)} %reshape.226), channel_id=1, replica_groups=mesh['tm'=16,'freq'=8] {'tm'}, dimensions={0} | all-to-all | bytes 8388608 | tf_op jit(solution)/shard_map/all_to_all | solution.py:91
  210.5 16.0 %reshape.227 = bf16[4096,2,8,32]{3,2,1,0:T(8,128)(2,1)} reshape(bf16[16,2,65536]{2,1,0:T(2,128)(2,1)} %all_to_all.51) | data formatting | bytes 8388608
  226.5 19.5 %copy.22 = bf16[2,32,16,8,256]{4,3,2,0,1:T(8,128)(2,1)} copy(bf16[2,32,16,8,256]{1,3,0,4,2:T(8,128)(2,1)} %bitcast.75) | data formatting | bytes 8388608 | tf_op jit(solution)/shard_map/all_to_all | solution.py:91
  246.0 0.0 copy-start
  246.0 5.7 %all-to-all-start.2 = ((bf16[2,32,128,256]{3,2,0,1:T(8,128)(2,1)}), bf16[2,32,128,256]{3,2,0,1:T(8,128)(2,1)}, u32[]{:S(2)}, u32[]{:S(2)}) async-start(bf16[2,32,128,256]{3,2,0,1:T(8,128)(2,1)} %bitcast.76), calls=%async_computation.2 | async-start | bytes 8388608 | tf_op jit(solution)/shard_map/all_to_all | solution.py:95
  251.7 0.0 copy-done
  251.8 5.9 %fusion.151 = (bf16[4,512,1024]{2,1,0:T(8,128)(2,1)}, bf16[4,512,1024]{2,1,0:T(8,128)(2,1)}) fusion(bf16[4,1024,1024]{2,1,0:T(8,128)(2,1)} %param.13), kind=kLoop, calls=%fused_computation.234 | loop fusion | bytes 16777216 | tf_op jit(solution)/shard_map/jit(_take)/gather | solution.py:90
  257.6 5.0 %gather_fusion = bf16[4,512,1024]{2,1,0:T(8,128)(2,1)} fusion(bf16[4,512,1024]{2,1,0:T(8,128)(2,1)} %get-tuple-element.7, s32[1024]{0:T(1024)S(1)} %pad_clamp_fusion), kind=kCustom, calls=%fused_computation | custom fusion | bytes 8388624 | tf_op jit(solution)/shard_map/jit(_take)/gather | solution.py:90
  262.6 5.0 %gather_fusion.1 = bf16[4,512,1024]{2,1,0:T(8,128)(2,1)} fusion(bf16[4,512,1024]{2,1,0:T(8,128)(2,1)} %get-tuple-element.8, s32[1024]{0:T(1024)S(1)} %pad_clamp_fusion), kind=kCustom, calls=%fused_computation.1 | custom fusion | bytes 8388624 | tf_op jit(solution)/shard_map/jit(_take)/gather | solution.py:90
  267.6 43.1 %all-to-all-done.2 = bf16[2,32,128,256]{3,2,0,1:T(8,128)(2,1)} async-done(((bf16[2,32,128,256]{3,2,0,1:T(8,128)(2,1)}), bf16[2,32,128,256]{3,2,0,1:T(8,128)(2,1)}, u32[]{:S(2)}, u32[]{:S(2)}) %all-to-all-start.2) | async-done | bytes 4194336 | tf_op jit(solution)/shard_map/all_to_all | solution.py:95
  310.7 7.5 %copy.24 = bf16[2,4,8,128,256]{3,2,4,0,1:T(8,128)(2,1)} copy(bf16[2,4,8,128,256]{4,3,0,1,2:T(8,128)(2,1)} %bitcast.26) | data formatting | bytes 8388608 | tf_op jit(solution)/shard_map/all_to_all | solution.py:95
  318.2 7.3 %all_to_all.47 = bf16[2,4,1024,256]{2,3,0,1:T(8,128)(2,1)} reshape(bf16[2,4,8,128,256]{3,2,4,0,1:T(8,128)(2,1)} %copy.24) | data formatting | bytes 8388608 | tf_op jit(solution)/shard_map/all_to_all | solution.py:95
  325.5 11.2 %convert_bitcast_fusion = bf16[2,4,1024,256]{2,3,0,1:T(8,128)(2,1)} fusion(bf16[2,4,1024,256]{2,3,0,1:T(8,128)(2,1)} %all_to_all.47, bf16[4,512,1024]{2,1,0:T(8,128)(2,1)} %gather_fusion.1, bf16[4,512,1024]{2,1,0:T(8,128)(2,1)} %gather_fusion, pred[4]{0:T(512)(128)(4,1)S(1)} %and_bitcast_fusion), kind=kOutput, calls=%fused_computation.19 | convolution fusion | flops 4318035968 | bytes 16777220 | tf_op jit(solution)/shard_map/bgf,cbfm->cbgm/dot_general | solution.py:92
  336.7 6.2 %copy.25 = bf16[2,4,1024,256]{3,2,1,0:T(8,128)(2,1)} copy(bf16[2,4,1024,256]{2,3,0,1:T(8,128)(2,1)} %convert_bitcast_fusion) | data formatting | bytes 8388608 | tf_op jit(solution)/shard_map/convert_element_type | solution.py:97
  (4 shorter events, 0.0 us)
Async XLA Ops:
  1.3 7.6 %collective-permute-start = (f32[128,16]{1,0:T(8,128)S(1)}, f32[128,16]{1,0:T(8,128)S(1)}, u32[]{:S(2)}, u32[]{:S(2)}) collective-permute-start(f32[128,16]{1,0:T(8,128)S(1)} %get-tuple-element.11), channel_id=1, source_target_pairs={{0,8},{8,16},{16,24},{24,32},{32,40},{40,48},{48,56},{56,64},{64,7... | collective-permute-start | bytes 24584 | tf_op jit(solution)/shard_map/ppermute | solution.py:17
  1.3 7.6 %collective-permute-start.1 = (f32[128,16]{1,0:T(8,128)S(1)}, f32[128,16]{1,0:T(8,128)S(1)}, u32[]{:S(2)}, u32[]{:S(2)}) collective-permute-start(f32[128,16]{1,0:T(8,128)S(1)} %get-tuple-element.12), channel_id=1, source_target_pairs={{8,0},{16,8},{24,16},{32,24},{40,32},{48,40},{56,48},{64,56},{72,6... | collective-permute-start | bytes 24584 | tf_op jit(solution)/shard_map/ppermute | solution.py:18
  17.7 59.3 %all-to-all-start = ((bf16[2,32,128,256]{3,1,0,2:T(8,128)(2,1)}), bf16[2,32,128,256]{3,1,0,2:T(8,128)(2,1)}, u32[]{:S(2)}, u32[]{:S(2)}) async-start(bf16[2,32,128,256]{3,1,0,2:T(8,128)(2,1)} %multiply_convert_fusion), calls=%async_computation | async-start | bytes 8388608 | tf_op jit(solution)/shard_map/all_to_all | solution.py:88
  246.0 5.7 %copy-start = (s32[4,1]{0,1:T(1,128)S(1)}, s32[4,1]{0,1:T(1,128)}, u32[]{:S(2)}) copy-start(s32[4,1]{0,1:T(1,128)} %param.12) | copy-start | bytes 52
  246.0 64.7 %all-to-all-start.2 = ((bf16[2,32,128,256]{3,2,0,1:T(8,128)(2,1)}), bf16[2,32,128,256]{3,2,0,1:T(8,128)(2,1)}, u32[]{:S(2)}, u32[]{:S(2)}) async-start(bf16[2,32,128,256]{3,2,0,1:T(8,128)(2,1)} %bitcast.76), calls=%async_computation.2 | async-start | bytes 8388608 | tf_op jit(solution)/shard_map/all_to_all | solution.py:95
where the time goes:
time: 345 us; the launch traced here: 343 us
  local copies, waits for them, and re-layouts  116 us (34%)
  waiting for transfers between devices  95.1 us (28%)
  blocking collectives  65 us (19%)
  matrix products  32.1 us (9%)
  starting transfers between devices  18.3 us (5%)
  other arithmetic  16 us (5%)
    all_to_all x1, blocking collectives, shards(): lax.all_to_all(spectrum, 'tm', split_axis=3, concat_axis=2, tiled=True)  65 us
    all_to_all x1, waiting for transfers between devices, shards(): lax.all_to_all(weighted, 'tm', split_axis=2, concat_axis=3, tiled=True)  50.1 us
    all_to_all x1, waiting for transfers between devices, shards(): lax.all_to_all(moved, 'freq', split_axis=1, concat_axis=2, tiled=True)  43.1 us
    unnamed x4, local copies, waits for them, and re-layouts  36.8 us
    convert_element_type x1, local copies, waits for them, and re-layouts, sidereal_transform(): return finished.astype(jnp.bfloat16)  23.2 us
    all_to_all x1, local copies, waits for them, and re-layouts, shards(): lax.all_to_all(spectrum, 'tm', split_axis=3, concat_axis=2, tiled=True)  19.5 us
    gather x3, local copies, waits for them, and re-layouts, shards(): chosen = jnp.take(filter_bank, baseline_delay_class[:, 0], axis=0)  15.8 us
    all_to_all x2, local copies, waits for them, and re-layouts, shards(): lax.all_to_all(moved, 'freq', split_axis=1, concat_axis=2, tiled=True)  14.8 us
  transfers between devices with their start and end apart: 4, of which 3 were waited for; matrix products, arithmetic and copies ran while one was open for 5% of the time, Pallas kernels for 0%

commit v1 on v0

--- a/solution.py
+++ b/solution.py
@@ -92,7 +92,12 @@
     return jnp.einsum(
         "bgf,cbfm->cbgm",
         chosen,
-        lax.all_to_all(moved, "freq", split_axis=1, concat_axis=2, tiled=True),
+        jnp.concatenate(
+            lax.all_to_all(
+                jnp.stack(jnp.split(moved, lax.axis_size("freq"), axis=1)), "freq", 0, 0
+            ),
+            axis=2,
+        ),
         preferred_element_type=jnp.float32,
     ).astype(jnp.bfloat16)
 

time: 345 us -> 356 us (1.032)
  local copies, waits for them, and re-layouts: 116 us -> 128 us
    all_to_all x2 -> x0, local copies, waits for them, and re-layouts: 14.8 us -> none  [shards(): lax.all_to_all(moved, 'freq', split_axis=1, concat_axis=2, tiled=True)]
    reshape x0 -> x2, local copies, waits for them, and re-layouts: none -> 14.8 us  [shards(): jnp.concatenate(lax.all_to_all(jnp.stack(jnp.split(moved, lax.axis_size('...]
    unnamed x4 -> x13, local copies, waits for them, and re-layouts: 36.8 us -> 47 us
where the time goes in v1:
time: 356 us; the launch traced here: 354 us
  local copies, waits for them, and re-layouts  128 us (36%)
  waiting for transfers between devices  95 us (27%)
  blocking collectives  65 us (18%)
  matrix products  32.1 us (9%)
  starting transfers between devices  18.3 us (5%)
  other arithmetic  16 us (4%)
    all_to_all x1, blocking collectives, shards(): lax.all_to_all(spectrum, 'tm', split_axis=3, concat_axis=2, tiled=True)  65 us
    all_to_all x1, waiting for transfers between devices, shards(): lax.all_to_all(weighted, 'tm', split_axis=2, concat_axis=3, tiled=True)  50.1 us
    unnamed x13, local copies, waits for them, and re-layouts  47 us
    all_to_all x1, waiting for transfers between devices, shards(): lax.all_to_all(jnp.stack(jnp.split(moved, lax.axis_size('freq'), axis=1))...  43 us
    convert_element_type x1, local copies, waits for them, and re-layouts, sidereal_transform(): return finished.astype(jnp.bfloat16)  23.2 us
    all_to_all x1, local copies, waits for them, and re-layouts, shards(): lax.all_to_all(spectrum, 'tm', split_axis=3, concat_axis=2, tiled=True)  19.5 us
    gather x3, local copies, waits for them, and re-layouts, shards(): chosen = jnp.take(filter_bank, baseline_delay_class[:, 0], axis=0)  15.9 us
    reshape x2, local copies, waits for them, and re-layouts, shards(): jnp.concatenate(lax.all_to_all(jnp.stack(jnp.split(moved, lax.axis_size('...  14.8 us
  transfers between devices with their start and end apart: 4, of which 3 were waited for; matrix products, arithmetic and copies ran while one was open for 5% of the time, Pallas kernels for 0%

profile of v1, /device:TPU:0, one launch (start us, length us, event | category | flops | bytes accessed | tf_op | source)
XLA Modules:
  0.0 354.0 jit_solution(11935213101935556060)
XLA Ops:
  0.0 1.2 exponential_multiply_fusion
  1.2 0.1 fusion.160
  1.3 0.0 collective-permute-start
  1.3 5.7 %collective-permute-start.1 = (f32[128,16]{1,0:T(8,128)S(1)}, f32[128,16]{1,0:T(8,128)S(1)}, u32[]{:S(2)}, u32[]{:S(2)}) collective-permute-start(f32[128,16]{1,0:T(8,128)S(1)} %get-tuple-element.12), channel_id=1, source_target_pairs={{8,0},{16,8},{24,16},{32,24},{40,32},{48,40},{56,48},{64,56},{72,6... | collective-permute-start | bytes 24584 | tf_op jit(solution)/shard_map/ppermute | solution.py:18
  7.0 1.9 collective-permute-done
  8.8 0.0 collective-permute-done.1
  8.9 1.7 fusion.41
  10.6 7.2 %multiply_convert_fusion = bf16[2,32,128,256]{3,1,0,2:T(8,128)(2,1)} fusion(bf16[2,32,128,256]{3,2,1,0:T(8,128)(2,1)} %param.7, f32[128,256]{1,0:T(8,128)S(1)} %fusion.41), kind=kLoop, calls=%fused_computation.13 | loop fusion | flops 6291456 | bytes 8519680 | tf_op jit(solution)/shard_map/convert_element_type | solution.py:86
  17.7 6.8 %all-to-all-start = ((bf16[2,32,128,256]{3,1,0,2:T(8,128)(2,1)}), bf16[2,32,128,256]{3,1,0,2:T(8,128)(2,1)}, u32[]{:S(2)}, u32[]{:S(2)}) async-start(bf16[2,32,128,256]{3,1,0,2:T(8,128)(2,1)} %multiply_convert_fusion), calls=%async_computation | async-start | bytes 8388608 | tf_op jit(solution)/shard_map/all_to_all | solution.py:88
  24.6 0.1 fusion.153
  24.6 0.1 fusion.151
  24.7 0.1 fusion.146
  24.8 1.0 fusion.134
  25.8 1.0 fusion.132
  26.8 0.1 maximum_bitcast_fusion.2
  26.9 50.1 %all-to-all-done = bf16[2,32,128,256]{3,1,0,2:T(8,128)(2,1)} async-done(((bf16[2,32,128,256]{3,1,0,2:T(8,128)(2,1)}), bf16[2,32,128,256]{3,1,0,2:T(8,128)(2,1)}, u32[]{:S(2)}, u32[]{:S(2)}) %all-to-all-start) | async-done | bytes 4194336 | tf_op jit(solution)/shard_map/all_to_all | solution.py:88
  77.0 9.8 %fusion.15 = f32[2,32,8,16,256]{4,3,2,1,0:T(8,128)S(1)} fusion(bf16[2,32,16,8,256]{4,1,0,3,2:T(8,128)(2,1)} %bitcast.8, f32[1,2,16,16]{3,2,1,0:T(8,128)S(1)} %get-tuple-element.14, f32[1,2,16,16]{3,2,1,0:T(8,128)S(1)} %get-tuple-element.13), kind=kOutput, calls=%fused_computation.23 | convolution fusion | flops 402654208 | bytes 12587008 | tf_op jit(solution)/shard_map/cbfps,dcjp->dbfjs/dot_general | solution.py:52
  86.8 1.9 multiply_add_fusion
  88.7 1.8 pad_maximum_fusion
  90.5 11.1 %fusion.10 = bf16[2,32,8,256,16]{3,1,4,2,0:T(8,128)(2,1)} fusion(f32[2,32,8,16,256]{4,3,2,1,0:T(8,128)S(1)} %pad_maximum_fusion, f32[1,2,256,256]{3,2,1,0:T(8,128)S(1)} %get-tuple-element.10, f32[1,2,256,256]{3,2,1,0:T(8,128)S(1)} %get-tuple-element.9), kind=kOutput, calls=%fused_computation.15 | convolution fusion | flops 6446907392 | bytes 13631488 | tf_op jit(solution)/shard_map/cbfjs,dcks->dbfkj/dot_general | solution.py:58
  101.6 23.2 %copy.41 = bf16[2,32,8,256,16]{1,2,0,4,3:T(8,128)(2,1)} copy(bf16[2,32,8,256,16]{3,1,4,2,0:T(8,128)(2,1)} %fusion.10) | data formatting | bytes 8388608 | tf_op jit(solution)/shard_map/convert_element_type | solution.py:61
  124.8 20.7 %reshape.234 = bf16[16,2,65536]{2,1,0:T(2,128)(2,1)} reshape(bf16[4096,2,8,32]{3,2,1,0:T(8,128)(2,1)} %bitcast.105) | data formatting | bytes 8388608
  145.5 65.0 %all_to_all.38 = bf16[16,2,65536]{2,1,0:T(2,128)(2,1)} all-to-all(bf16[16,2,65536]{2,1,0:T(2,128)(2,1)} %reshape.234), channel_id=1, replica_groups=mesh['tm'=16,'freq'=8] {'tm'}, dimensions={0} | all-to-all | bytes 8388608 | tf_op jit(solution)/shard_map/all_to_all | solution.py:91
  210.5 16.1 %reshape.235 = bf16[4096,2,8,32]{3,2,1,0:T(8,128)(2,1)} reshape(bf16[16,2,65536]{2,1,0:T(2,128)(2,1)} %all_to_all.38) | data formatting | bytes 8388608
  226.6 19.5 %copy.31 = bf16[2,32,16,8,256]{4,3,2,1,0:T(8,128)(2,1)} copy(bf16[2,32,16,8,256]{1,3,0,4,2:T(8,128)(2,1)} %bitcast.106) | data formatting | bytes 8388608 | tf_op jit(solution)/shard_map/all_to_all | solution.py:91
  246.0 0.0 copy-start
  246.0 2.0 fusion.31
  248.1 1.9 fusion.30
  249.9 1.9 fusion.29
  251.8 1.9 fusion.28
  253.7 0.0 copy-done
  253.7 0.8 fusion.27
  254.6 0.8 fusion.26
  255.4 0.8 fusion.25
  256.3 0.8 fusion.24
  257.1 0.0 copy-start.1
  257.1 5.7 %all-to-all-start.2 = ((bf16[8,2,4,128,256]{4,3,2,1,0:T(8,128)(2,1)}), bf16[8,2,4,128,256]{4,3,2,1,0:T(8,128)(2,1)}, u32[]{:S(2)}, u32[]{:S(2)}) async-start(bf16[8,2,4,128,256]{4,3,2,1,0:T(8,128)(2,1)} %fusion.24), calls=%async_computation.2 | async-start | bytes 8388608 | tf_op jit(solution)/shard_map/all_to_all | solution.py:96
  262.8 0.0 copy-done.1
  262.9 6.0 %fusion.159 = (bf16[4,512,1024]{2,1,0:T(8,128)(2,1)}, bf16[4,512,1024]{2,1,0:T(8,128)(2,1)}) fusion(bf16[4,1024,1024]{2,1,0:T(8,128)(2,1)} %param.13), kind=kLoop, calls=%fused_computation.250 | loop fusion | bytes 16777216 | tf_op jit(solution)/shard_map/jit(_take)/gather | solution.py:90
  268.9 5.0 %gather_fusion = bf16[4,512,1024]{2,1,0:T(8,128)(2,1)} fusion(bf16[4,512,1024]{2,1,0:T(8,128)(2,1)} %get-tuple-element.7, s32[1024]{0:T(1024)S(1)} %pad_clamp_fusion), kind=kCustom, calls=%fused_computation | custom fusion | bytes 8388624 | tf_op jit(solution)/shard_map/jit(_take)/gather | solution.py:90
  273.8 5.0 %gather_fusion.1 = bf16[4,512,1024]{2,1,0:T(8,128)(2,1)} fusion(bf16[4,512,1024]{2,1,0:T(8,128)(2,1)} %get-tuple-element.8, s32[1024]{0:T(1024)S(1)} %pad_clamp_fusion), kind=kCustom, calls=%fused_computation.1 | custom fusion | bytes 8388624 | tf_op jit(solution)/shard_map/jit(_take)/gather | solution.py:90
  278.8 43.0 %all-to-all-done.2 = bf16[8,2,4,128,256]{4,3,2,1,0:T(8,128)(2,1)} async-done(((bf16[8,2,4,128,256]{4,3,2,1,0:T(8,128)(2,1)}), bf16[8,2,4,128,256]{4,3,2,1,0:T(8,128)(2,1)}, u32[]{:S(2)}, u32[]{:S(2)}) %all-to-all-start.2) | async-done | bytes 4194336 | tf_op jit(solution)/shard_map/all_to_all | solution.py:96
  321.8 7.5 %copy.32 = bf16[2,4,8,128,256]{3,2,4,0,1:T(8,128)(2,1)} copy(bf16[2,4,8,128,256]{4,3,1,0,2:T(8,128)(2,1)} %bitcast.34) | data formatting | bytes 8388608 | tf_op jit(solution)/shard_map/reshape | solution.py:95
  329.3 7.3 %reshape.210 = bf16[2,4,1024,256]{2,3,0,1:T(8,128)(2,1)} reshape(bf16[2,4,8,128,256]{3,2,4,0,1:T(8,128)(2,1)} %copy.32) | data formatting | bytes 8388608 | tf_op jit(solution)/shard_map/reshape | solution.py:95
  336.5 11.2 %convert_bitcast_fusion = bf16[2,4,1024,256]{2,3,0,1:T(8,128)(2,1)} fusion(bf16[2,4,1024,256]{2,3,0,1:T(8,128)(2,1)} %reshape.210, bf16[4,512,1024]{2,1,0:T(8,128)(2,1)} %gather_fusion.1, bf16[4,512,1024]{2,1,0:T(8,128)(2,1)} %gather_fusion, pred[4]{0:T(512)(128)(4,1)S(1)} %and_bitcast_fusion), kind=kOutput, calls=%fused_computation.19 | convolution fusion | flops 4318035968 | bytes 16777220 | tf_op jit(solution)/shard_map/bgf,cbfm->cbgm/dot_general | solution.py:92
  347.7 6.2 %copy.33 = bf16[2,4,1024,256]{3,2,1,0:T(8,128)(2,1)} copy(bf16[2,4,1024,256]{2,3,0,1:T(8,128)(2,1)} %convert_bitcast_fusion) | data formatting | bytes 8388608 | tf_op jit(solution)/shard_map/convert_element_type | solution.py:102
  (4 shorter events, 0.0 us)
Async XLA Ops:
  1.3 7.6 %collective-permute-start = (f32[128,16]{1,0:T(8,128)S(1)}, f32[128,16]{1,0:T(8,128)S(1)}, u32[]{:S(2)}, u32[]{:S(2)}) collective-permute-start(f32[128,16]{1,0:T(8,128)S(1)} %get-tuple-element.11), channel_id=1, source_target_pairs={{0,8},{8,16},{16,24},{24,32},{32,40},{40,48},{48,56},{56,64},{64,7... | collective-permute-start | bytes 24584 | tf_op jit(solution)/shard_map/ppermute | solution.py:17
  1.3 7.6 %collective-permute-start.1 = (f32[128,16]{1,0:T(8,128)S(1)}, f32[128,16]{1,0:T(8,128)S(1)}, u32[]{:S(2)}, u32[]{:S(2)}) collective-permute-start(f32[128,16]{1,0:T(8,128)S(1)} %get-tuple-element.12), channel_id=1, source_target_pairs={{8,0},{16,8},{24,16},{32,24},{40,32},{48,40},{56,48},{64,56},{72,6... | collective-permute-start | bytes 24584 | tf_op jit(solution)/shard_map/ppermute | solution.py:18
  17.7 59.3 %all-to-all-start = ((bf16[2,32,128,256]{3,1,0,2:T(8,128)(2,1)}), bf16[2,32,128,256]{3,1,0,2:T(8,128)(2,1)}, u32[]{:S(2)}, u32[]{:S(2)}) async-start(bf16[2,32,128,256]{3,1,0,2:T(8,128)(2,1)} %multiply_convert_fusion), calls=%async_computation | async-start | bytes 8388608 | tf_op jit(solution)/shard_map/all_to_all | solution.py:88
  246.0 7.7 %copy-start = (bf16[2,32,16,8,256]{4,3,2,1,0:T(8,128)(2,1)S(1)}, bf16[2,32,16,8,256]{4,3,2,1,0:T(8,128)(2,1)}, u32[]{:S(2)}) copy-start(bf16[2,32,16,8,256]{4,3,2,1,0:T(8,128)(2,1)} %copy.31) | copy-start | bytes 12582916
  257.1 5.7 %copy-start.1 = (s32[4,1]{0,1:T(1,128)S(1)}, s32[4,1]{0,1:T(1,128)}, u32[]{:S(2)}) copy-start(s32[4,1]{0,1:T(1,128)} %param.12) | copy-start | bytes 52
  257.1 64.7 %all-to-all-start.2 = ((bf16[8,2,4,128,256]{4,3,2,1,0:T(8,128)(2,1)}), bf16[8,2,4,128,256]{4,3,2,1,0:T(8,128)(2,1)}, u32[]{:S(2)}, u32[]{:S(2)}) async-start(bf16[8,2,4,128,256]{4,3,2,1,0:T(8,128)(2,1)} %fusion.24), calls=%async_computation.2 | async-start | bytes 8388608 | tf_op jit(solution)/shard_map/all_to_all | solution.py:96
